TPU v7x, 32 devices: a whole 2x2x4 slice. The times are simulated.
32 devices in a mesh: seg: 8 (over z, x), mp: 4 (over y, core).
Axes of the slice: x: 2, y: 2, z: 4, core: 2. Of those that a mesh axis runs over, the one named last changes fastest.
Arguments:
- patches: bfloat16 [8192, 768], P('seg'), may hold values from -6 to 6
- curve_owner: int32 [8192], P('seg'), may hold values from 0 to 7, as said below
- arrival_slot: int32 [8192], P('seg'), may hold values from 0 to 2047, as said below
- patch_level: int32 [8192], P('seg'), may hold values from 0 to 3
- neighbours: int32 [8192, 16], P('seg'), may hold values from 0 to 8191, as said below
- level_embed: bfloat16 [4, 768], replicated, may hold values from -3 to 3
- norm_gain: float32 [768], replicated, may hold values from 0.5 to 2
- qkv_weight: bfloat16 [768, 3, 768], P(None, None, 'mp')
- out_weight: bfloat16 [768, 768], P('mp'), may hold values from -0.21875 to 0.21875
- cotangent: bfloat16 [8192, 768], P('seg'), may hold values from -6 to 6
Outputs:
- token_grads: float32 [8192, 768], P('seg', 'mp')
- qkv_grad: float32 [768, 3, 768], P(None, None, 'mp')
- out_grad: float32 [768, 768], P('mp')
- gain_grad: float32 [768], P('mp')
Inputs may be any that keep to these rules, and one draw needn't show every extreme that they name: `curve_owner`: every device owns exactly 1024 patches. No device holds more than 256 patches with one owner, and in every draw some device holds exactly 256 patches with some owner. `arrival_slot`: entry d * 1024 + p is s * 256 + k: the patch at position p of owner d is the k-th, counted from 0 in row order, of the rows of device s whose owner is d. The entries of one owner are distinct and name every patch it owns. `neighbours`: row p lists positions within 128 of p on the curve, p itself among them; a position may repeat.
All inputs are finite; a program needn't handle non-finite values.
Results may differ from a plain program's by a relative error of at most 0.029.
Values may be sent and summed in bfloat16 or wider, within the bound.
A program may use at most 64 MiB of HBM per device.

v0:
```python
import jax
import jax.numpy as jnp
from jax import lax
from jax.sharding import PartitionSpec as P

DH = 64
R = 128
EPSILON = 1e-06


def with_halo(cells, sides, width):
    for axis, dim in sides:
        count = lax.axis_size(axis)
        ends = count - 1
        head = lax.slice_in_dim(cells, 0, width, axis=dim)
        tail = lax.slice_in_dim(cells, cells.shape[dim] - width, cells.shape[dim], axis=dim)
        cells = jnp.concatenate(
            [
                lax.ppermute(tail, axis, [(i, (i + 1) % count) for i in range(ends)]),
                cells,
                lax.ppermute(head, axis, [((i + 1) % count, i) for i in range(ends)]),
            ],
            axis=dim,
        )
    return cells


def per_device(
    patches,
    curve_owner,
    arrival_slot,
    patch_level,
    neighbours,
    level_embed,
    norm_gain,
    qkv_weight,
    out_weight,
    cotangent,
):
    segments = lax.axis_size("seg")
    shares = lax.axis_size("mp")
    tok_rows = patches.shape[0]
    model_width = patches.shape[1]
    local_width = qkv_weight.shape[2]
    heads_here = local_width // DH
    capacity = 2 * tok_rows // segments
    share_width = model_width // shares
    first_column = lax.axis_index("mp") * share_width
    onehot = (curve_owner[:, None] == jnp.arange(segments, dtype=jnp.int32)[None, :]).astype(
        jnp.int32
    )
    row_ranks = jnp.sum(onehot * (jnp.cumsum(onehot, axis=0) - onehot), axis=1)
    slot_index = curve_owner * capacity + row_ranks
    columns_here = patches.shape[1]
    buffer = (
        jnp.zeros((segments * capacity, columns_here), patches.dtype).at[slot_index].set(patches)
    )
    arrived = lax.all_to_all(
        buffer.reshape(segments, capacity, columns_here),
        "seg",
        split_axis=0,
        concat_axis=0,
        tiled=True,
    )
    routed = arrived.reshape(segments * capacity, columns_here)[arrival_slot]
    levels_count = level_embed.shape[0]
    level_hot = (patch_level[:, None] == jnp.arange(levels_count, dtype=jnp.int32)[None, :]).astype(
        jnp.bfloat16
    )
    embedded = routed.astype(jnp.float32) + jnp.dot(
        level_hot, level_embed, preferred_element_type=jnp.float32
    )
    inv_rms = lax.rsqrt(jnp.mean(embedded * embedded, axis=1, keepdims=True) + EPSILON)
    normed = embedded * inv_rms
    hidden = (normed * norm_gain).astype(jnp.bfloat16)
    flat_weight = qkv_weight.reshape(model_width, 3 * local_width)
    project = jnp.dot(hidden, flat_weight, preferred_element_type=jnp.float32).astype(jnp.bfloat16)
    queries = project[:, :local_width]
    key_value = project[:, local_width:]
    extended = with_halo(key_value, (("seg", 0),), R)
    grad_out = lax.dot_general(
        cotangent, out_weight, (((1,), (1,)), ((), ())), preferred_element_type=jnp.float32
    ).astype(jnp.bfloat16)
    block_rows = min(tok_rows, 512)
    key_span = block_rows + 2 * R
    score_scale = DH ** (-0.5)
    first_key = lax.axis_index("seg") * tok_rows - R
    grad_ext = jnp.zeros((tok_rows + 2 * R, 2 * local_width), jnp.float32)
    outputs = []
    query_grads = []
    for block_index in range(tok_rows // block_rows):
        block_start = block_index * block_rows
        query_block = queries[block_start : block_start + block_rows].reshape(
            block_rows, heads_here, DH
        )
        pair_block = extended[block_start : block_start + key_span].reshape(
            key_span, 2, heads_here, DH
        )
        key_block = pair_block[:, 0]
        value_block = pair_block[:, 1]
        positions = first_key + block_start + jnp.arange(key_span, dtype=jnp.int32)
        listed = neighbours[block_start : block_start + block_rows]
        allowed = listed[:, 0:1] == positions[None, :]
        for column in range(1, listed.shape[1]):
            allowed = allowed | (listed[:, column : column + 1] == positions[None, :])
        allowed = allowed[None]
        scores = (
            jnp.einsum("qhd,khd->hqk", query_block, key_block, preferred_element_type=jnp.float32)
            * score_scale
        )
        row_top = jnp.max(jnp.where(allowed, scores, -jnp.inf), axis=2, keepdims=True)
        exponent = jnp.where(allowed, jnp.exp(scores - row_top), 0.0)
        probability = exponent / jnp.sum(exponent, axis=2, keepdims=True)
        weights = probability.astype(jnp.bfloat16)
        out_block = jnp.einsum(
            "hqk,khd->qhd", weights, value_block, preferred_element_type=jnp.float32
        ).astype(jnp.bfloat16)
        grad_block = grad_out[block_start : block_start + block_rows].reshape(
            block_rows, heads_here, DH
        )
        row_delta = jnp.sum(
            grad_block.astype(jnp.float32) * out_block.astype(jnp.float32), axis=2
        ).T[:, :, None]
        grad_prob = jnp.einsum(
            "qhd,khd->hqk", grad_block, value_block, preferred_element_type=jnp.float32
        )
        dscore = (probability * (grad_prob - row_delta) * score_scale).astype(jnp.bfloat16)
        dquery = jnp.einsum("hqk,khd->qhd", dscore, key_block, preferred_element_type=jnp.float32)
        grad_key = jnp.einsum(
            "hqk,qhd->khd", dscore, query_block, preferred_element_type=jnp.float32
        )
        dvalue = jnp.einsum("hqk,qhd->khd", weights, grad_block, preferred_element_type=jnp.float32)
        joined = jnp.concatenate(
            [grad_key.reshape(key_span, local_width), dvalue.reshape(key_span, local_width)], axis=1
        )
        grad_ext = grad_ext.at[block_start : block_start + key_span].add(joined)
        outputs.append(out_block.reshape(block_rows, local_width))
        query_grads.append(dquery.reshape(block_rows, local_width))
    rim_rows = jnp.concatenate([grad_ext[:R], grad_ext[tok_rows + R :]], axis=0)
    returned = with_halo(rim_rows, (("seg", 0),), R)
    grad_kv = (
        grad_ext[R : R + tok_rows]
        .at[:R]
        .add(returned[:R])
        .at[tok_rows - R :]
        .add(returned[3 * R :])
    )
    grad_qkv = jnp.concatenate([jnp.concatenate(query_grads, axis=0), grad_kv], axis=1).astype(
        jnp.bfloat16
    )
    attended = jnp.concatenate(outputs, axis=0)
    qkv_part = lax.dot_general(
        hidden, grad_qkv, (((0,), (0,)), ((), ())), preferred_element_type=jnp.float32
    )
    out_part = lax.dot_general(
        attended, cotangent, (((0,), (0,)), ((), ())), preferred_element_type=jnp.float32
    )
    hidden_part = lax.dot_general(
        grad_qkv, flat_weight, (((1,), (1,)), ((), ())), preferred_element_type=jnp.float32
    )
    grad_hidden = lax.psum(hidden_part, "mp")
    scaled = grad_hidden * norm_gain
    full_grads = cotangent.astype(jnp.float32) + inv_rms * (
        scaled - normed * jnp.mean(scaled * normed, axis=1, keepdims=True)
    )
    token_grads = lax.dynamic_slice_in_dim(full_grads, first_column, share_width, 1)
    gain_part = lax.dynamic_slice_in_dim(
        jnp.sum(grad_hidden * normed, axis=0), first_column, share_width, 0
    )
    summed_qkv, summed_out, summed_gain = lax.psum((qkv_part, out_part, gain_part), "seg")
    factor = (tok_rows * segments) ** (-0.5)
    qkv_grad = (summed_qkv * factor).reshape(model_width, 3, local_width)
    return (token_grads, qkv_grad, summed_out * factor, summed_gain * factor)


def solution(mesh):
    placed = (
        P("seg", None),
        P("seg"),
        P("seg"),
        P("seg"),
        P("seg", None),
        P(),
        P(),
        P(None, None, "mp"),
        P("mp", None),
        P("seg", None),
    )
    return jax.shard_map(
        per_device,
        mesh=mesh,
        in_specs=placed,
        out_specs=(P("seg", "mp"), P(None, None, "mp"), P("mp", None), P("mp")),
        check_vma=False,
    )
```

profile of v0, /device:TPU:0, one launch (start us, length us, event | category | flops | bytes accessed | tf_op | source)
XLA Modules:
  0.0 360.0 jit_solution(1146869149718708248)
XLA Ops:
  8.0 2.3 reduce-window.6
  12.2 7.9 %scatter_custom_fusion = bf16[2048,768]{1,0:T(8,128)(2,1)} fusion(s32[1024]{0:T(1024)S(1)} %compare_select_fusion.1, bf16[1024,768]{1,0:T(8,128)(2,1)} %param.18, bf16[]{:T(256)} %constant.136.clone.1), kind=kCustom, calls=%fused_computation.33 | custom fusion | bytes 3146240 | tf_op jit(solution)/shard_map/scatter | solution.py:56
  20.1 7.4 %all-to-all-start = ((bf16[8,256,768]{2,1,0:T(8,128)(2,1)}), bf16[8,256,768]{2,1,0:T(8,128)(2,1)}, u32[]{:S(2)}, u32[]{:S(2)}) async-start(bf16[8,256,768]{2,1,0:T(8,128)(2,1)} %bitcast.153), calls=%async_computation | async-start | bytes 6291456 | tf_op jit(solution)/shard_map/all_to_all | solution.py:58
  29.1 4.8 %compare_or_fusion = pred[512,768]{1,0:T(8,128)(4,1)} fusion(s32[768]{0:T(1024)S(1)} %iota_add_fusion, s32[512]{0:T(512)S(1)} %bitcast.222, s32[512]{0:T(512)S(1)} %bitcast.221, s32[512]{0:T(512)S(1)} %bitcast.197, s32[512]{0:T(512)S(1)} %bitcast.198, s32[512]{0:T(512)S(1)} %bitcast.199, s32[512]{0:T(512)S(1)} %bitcast.200, s32[512]{0:T(512)S(1)} %bitcast.201, ...), kind=kLoop, calls=%fused_computation.35 | loop fusion | flops 12189696 | bytes 429056 | tf_op jit(solution)/shard_map/or | solution.py:105
  33.9 4.8 %compare_or_fusion.1 = pred[512,768]{1,0:T(8,128)(4,1)} fusion(s32[768]{0:T(1024)S(1)} %iota_add_fusion.1, s32[512]{0:T(512)S(1)} %bitcast.191, s32[512]{0:T(512)S(1)} %bitcast.192, s32[512]{0:T(512)S(1)} %bitcast.193, s32[512]{0:T(512)S(1)} %bitcast.194, s32[512]{0:T(512)S(1)} %bitcast.195, s32[512]{0:T(512)S(1)} %bitcast.210, s32[512]{0:T(512)S(1)} %bitcast.211, ...), kind=kLoop, calls=%fused_computation.36 | loop fusion | flops 12189696 | bytes 429056 | tf_op jit(solution)/shard_map/or | solution.py:105
  38.6 59.7 %all-to-all-done = bf16[8,256,768]{2,1,0:T(8,128)(2,1)} async-done(((bf16[8,256,768]{2,1,0:T(8,128)(2,1)}), bf16[8,256,768]{2,1,0:T(8,128)(2,1)}, u32[]{:S(2)}, u32[]{:S(2)}) %all-to-all-start) | async-done | bytes 3145760 | tf_op jit(solution)/shard_map/all_to_all | solution.py:58
  98.3 7.9 %gather_fusion = bf16[1024,768]{1,0:T(8,128)(2,1)} fusion(bf16[2048,768]{1,0:T(8,128)(2,1)} %bitcast.3, s32[1024]{0:T(1024)S(1)} %fusion.43), kind=kCustom, calls=%fused_computation | custom fusion | bytes 3149824 | tf_op jit(solution)/shard_map/gather | solution.py:65
  106.2 1.7 copy.18
  113.0 4.7 %collective-permute-start = (bf16[128,384]{0,1:T(8,128)(2,1)S(1)}, bf16[128,384]{0,1:T(8,128)(2,1)S(1)}, u32[]{:S(2)}, u32[]{:S(2)}) collective-permute-start(bf16[128,384]{0,1:T(8,128)(2,1)S(1)} %get-tuple-element.62), channel_id=1, source_target_pairs={{0,4},{4,8},{8,12},{12,16},{16,20},{20,24},{24,28},{1,5},{5,9},{9,... | collective-permute-start | bytes 294920 | tf_op jit(solution)/shard_map/ppermute | solution.py:19
  119.9 5.7 %fusion.57 = (f32[3,512]{1,0:T(4,128)S(1)}, f32[3,512,768]{2,1,0:T(8,128)}) fusion(pred[512,768]{1,0:T(8,128)(4,1)} %compare_or_fusion.1, bf16[512,3,64]{0,2,1:T(8,128)(2,1)S(1)} %bitcast.181, bf16[768,2,3,64]{0,3,2,1:T(8,128)(2,1)S(1)} %bitcast.164), kind=kOutput, calls=%fused_computation.108 | convolution fusion | flops 309068544 | bytes 6494208 | tf_op jit(solution)/shard_map/sub | solution.py:112
  125.6 2.7 fusion.17
  131.2 5.7 %fusion.58 = (f32[3,512]{1,0:T(4,128)S(1)}, f32[3,512,768]{2,1,0:T(8,128)}) fusion(pred[512,768]{1,0:T(8,128)(4,1)} %compare_or_fusion, bf16[512,3,64]{0,2,1:T(8,128)(2,1)} %bitcast.179, bf16[768,2,3,64]{0,3,2,1:T(8,128)(2,1)S(1)} %bitcast.160), kind=kOutput, calls=%fused_computation.109 | convolution fusion | flops 309068544 | bytes 6494208 | tf_op jit(solution)/shard_map/sub | solution.py:112
  136.9 2.8 fusion.18
  147.2 4.3 %collective-permute-start.2 = (f32[128,384]{0,1:T(8,128)S(1)}, f32[128,384]{0,1:T(8,128)S(1)}, u32[]{:S(2)}, u32[]{:S(2)}) collective-permute-start(f32[128,384]{0,1:T(8,128)S(1)} %slice.336), channel_id=1, source_target_pairs={{0,4},{4,8},{8,12},{12,16},{16,20},{20,24},{24,28},{1,5},{5,9},{9,... | collective-permute-start | bytes 589832 | tf_op jit(solution)/shard_map/ppermute | solution.py:19
  152.6 2.1 collective-permute-done.2
  157.0 6.7 %collective-permute-done.3 = f32[128,384]{0,1:T(8,128)S(1)} collective-permute-done((f32[128,384]{0,1:T(8,128)S(1)}, f32[128,384]{0,1:T(8,128)S(1)}, u32[]{:S(2)}, u32[]{:S(2)}) %collective-permute-start.3) | collective-permute-done | bytes 196640 | tf_op jit(solution)/shard_map/ppermute | solution.py:21
  163.8 3.1 fusion.29
  169.3 4.3 %fusion.28 = f32[768,576]{0,1:T(8,128)} fusion(bf16[1024,384]{0,1:T(8,128)(2,1)S(1)} %convert.16, bf16[512,192]{0,1:T(8,128)(2,1)S(1)} %bitcast.186, bf16[512,192]{0,1:T(8,128)(2,1)S(1)} %bitcast.184, f32[1024,768]{0,1:T(8,128)} %copy-done.1, f32[768]{0:T(1024)S(1)} %copy-done.13), kind=kOutput, calls=%fused_computation.56 | convolution fusion | flops 911081472 | bytes 6097920 | tf_op jit(solution)/shard_map/dot_general | solution.py:152
  174.0 62.2 %all-reduce.5.cloned.1.call-done = f32[1024,768]{0,1:T(8,128)} async-done(((f32[1024,768]{0,1:T(8,128)}), f32[1024,768]{0,1:T(8,128)}) %all-reduce.5.cloned.1.call-update) | async-done | bytes 3145744 | tf_op jit(solution)/shard_map/psum | solution.py:161
  236.2 5.2 %multiply_reduce_fusion = (f32[768]{0:T(1024)S(1)}, f32[1024]{0:T(1024)S(1)}, f32[1024,768]{0,1:T(8,128)}) fusion(f32[1024,768]{0,1:T(8,128)} %all-reduce.5.cloned.1.call-done, f32[1024,768]{0,1:T(8,128)} %copy-done.1, f32[768]{0:T(1024)S(1)} %copy-done.13), kind=kLoop, calls=%fused_computation.14 | loop fusion | flops 3930368 | bytes 9447424 | tf_op jit(solution)/shard_map/reduce_sum | solution.py:168
  241.5 22.3 %psum.31 = f32[192]{0:T(256)S(1)} all-reduce(f32[192]{0:T(256)S(1)} %dynamic_slice.7), channel_id=1, replica_groups=mesh['seg'=8,'mp'=4] {'seg'}, use_global_device_ids=true, to_apply=%region_16.17 | all-reduce | flops 192 | bytes 1536 | tf_op jit(solution)/shard_map/psum | solution.py:170
  264.4 2.5 fusion.22
  266.9 82.6 %all-reduce.7.cloned.1.call-done = (f32[768,576]{0,1:T(8,128)}, f32[192,768]{1,0:T(8,128)}) async-done(((f32[768,576]{0,1:T(8,128)}, f32[192,768]{1,0:T(8,128)}), (f32[768,576]{0,1:T(8,128)}, f32[192,768]{1,0:T(8,128)})) %all-reduce.7.cloned.1.call-update) | async-done | bytes 2359312 | tf_op jit(solution)/shard_map/psum | solution.py:170
  349.4 2.9 broadcast_multiply_fusion.1
  (101 shorter events, 29.3 us)
Async XLA Ops:
  7.2 20.5 %copy-start = (bf16[1024,768]{1,0:T(8,128)(2,1)S(1)}, bf16[1024,768]{1,0:T(8,128)(2,1)}, u32[]{:S(2)}) copy-start(bf16[1024,768]{1,0:T(8,128)(2,1)} %param.27) | copy-start | bytes 4718596
  20.1 7.5 %copy-start.15 = (s32[1024]{0:T(1024)S(1)}, s32[1024]{0:T(1024)}, u32[]{:S(2)}) copy-start(s32[1024]{0:T(1024)} %param.20) | copy-start | bytes 12292
  20.1 7.5 %copy-start.11 = (s32[1024,16]{0,1:T(8,128)S(1)}, s32[1024,16]{0,1:T(8,128)}, u32[]{:S(2)}) copy-start(s32[1024,16]{0,1:T(8,128)} %param.22) | copy-start | bytes 196612
  20.1 7.6 %copy-start.18 = (bf16[192,768]{1,0:T(8,128)(2,1)S(1)}, bf16[192,768]{1,0:T(8,128)(2,1)}, u32[]{:S(2)}) copy-start(bf16[192,768]{1,0:T(8,128)(2,1)} %param.26) | copy-start | bytes 884740
  20.1 78.2 %all-to-all-start = ((bf16[8,256,768]{2,1,0:T(8,128)(2,1)}), bf16[8,256,768]{2,1,0:T(8,128)(2,1)}, u32[]{:S(2)}, u32[]{:S(2)}) async-start(bf16[8,256,768]{2,1,0:T(8,128)(2,1)} %bitcast.153), calls=%async_computation | async-start | bytes 6291456 | tf_op jit(solution)/shard_map/all_to_all | solution.py:58
  27.5 208.7 %all-reduce.5.cloned.1.call-start = ((), (), s32[]{:S(2)}) async-start(), calls=%async_computation.1 | async-start | bytes 6291456 | tf_op jit(solution)/shard_map/psum | solution.py:161
  106.2 1.8 copy-start.12
  106.2 1.8 copy-start.14
  110.1 1.6 copy-start.1
  111.7 6.8 %collective-permute-start.1 = (bf16[128,384]{0,1:T(8,128)(2,1)S(1)}, bf16[128,384]{0,1:T(8,128)(2,1)S(1)}, u32[]{:S(2)}, u32[]{:S(2)}) collective-permute-start(bf16[128,384]{0,1:T(8,128)(2,1)S(1)} %get-tuple-element.61), channel_id=1, source_target_pairs={{4,0},{8,4},{12,8},{16,12},{20,16},{24,20},{28,24},{5,1},{9,5},{13... | collective-permute-start | bytes 294920 | tf_op jit(solution)/shard_map/ppermute | solution.py:21
  113.0 6.8 %collective-permute-start = (bf16[128,384]{0,1:T(8,128)(2,1)S(1)}, bf16[128,384]{0,1:T(8,128)(2,1)S(1)}, u32[]{:S(2)}, u32[]{:S(2)}) collective-permute-start(bf16[128,384]{0,1:T(8,128)(2,1)S(1)} %get-tuple-element.62), channel_id=1, source_target_pairs={{0,4},{4,8},{8,12},{12,16},{16,20},{20,24},{24,28},{1,5},{5,9},{9,... | collective-permute-start | bytes 294920 | tf_op jit(solution)/shard_map/ppermute | solution.py:19
  118.5 7.1 %copy-start.8 = (bf16[512,192]{0,1:T(8,128)(2,1)}, bf16[512,192]{0,1:T(8,128)(2,1)S(1)}, u32[]{:S(2)}) copy-start(bf16[512,192]{0,1:T(8,128)(2,1)S(1)} %get-tuple-element.64) | copy-start | bytes 589828
  125.6 2.7 copy-start.3
  131.2 10.6 %slice-start = ((s8[4718592]{0:T(1024)(128)(4,1)}), s8[524288]{0:T(1024)(128)(4,1)S(1)}, s32[]{:S(2)}) async-start(s8[4718592]{0:T(1024)(128)(4,1)} %bitcast.154), calls=%async_computation.3 | async-start | bytes 1048576
  136.9 4.9 %slice-start.1 = ((s8[4718592]{0:T(1024)(128)(4,1)}), s8[4194304]{0:T(1024)(128)(4,1)S(1)}, s32[]{:S(2)}) async-start(s8[4718592]{0:T(1024)(128)(4,1)} %bitcast.154), calls=%async_computation.4 | async-start | bytes 8388608
  139.8 2.1 copy-start.4
  141.3 2.4 slice-start.2
  141.9 2.3 slice-start.3
  144.2 1.4 copy-start.7
  147.2 7.5 %collective-permute-start.2 = (f32[128,384]{0,1:T(8,128)S(1)}, f32[128,384]{0,1:T(8,128)S(1)}, u32[]{:S(2)}, u32[]{:S(2)}) collective-permute-start(f32[128,384]{0,1:T(8,128)S(1)} %slice.336), channel_id=1, source_target_pairs={{0,4},{4,8},{8,12},{12,16},{16,20},{20,24},{24,28},{1,5},{5,9},{9,... | collective-permute-start | bytes 589832 | tf_op jit(solution)/shard_map/ppermute | solution.py:19
  154.7 9.1 %copy-start.17 = (bf16[768,3,192]{0,2,1:T(8,128)(2,1)S(1)}, bf16[768,3,192]{0,2,1:T(8,128)(2,1)}, u32[]{:S(2)}) copy-start(bf16[768,3,192]{0,2,1:T(8,128)(2,1)} %param.25) | copy-start | bytes 2654212
  154.7 8.9 %collective-permute-start.3 = (f32[128,384]{0,1:T(8,128)S(1)}, f32[128,384]{0,1:T(8,128)S(1)}, u32[]{:S(2)}, u32[]{:S(2)}) collective-permute-start(f32[128,384]{0,1:T(8,128)S(1)} %get-tuple-element.59), channel_id=1, source_target_pairs={{4,0},{8,4},{12,8},{16,12},{20,16},{24,20},{28,24},{5,1},{9,5},{13... | collective-permute-start | bytes 589832 | tf_op jit(solution)/shard_map/ppermute | solution.py:21
  167.0 182.4 %all-reduce.7.cloned.1.call-start = ((), (), s32[]{:S(2)}) async-start(), calls=%async_computation.2 | async-start | bytes 4718592 | tf_op jit(solution)/shard_map/psum | solution.py:170
  349.4 2.9 copy-start.10
  (6 other events, 6.3 us)
Sparse Core Ops, SparseCore 0:
  167.1 69.0 all-reduce.4
  240.4 108.9 all-reduce.6
where the time goes:
time: 361 us; the launch traced here: 360 us
  waiting for transfers between devices  215 us (60%)
  other arithmetic  33.5 us (9%)
  matrix products  33.5 us (9%)
  local copies, waits for them, and re-layouts  22.3 us (6%)
  blocking collectives  22.3 us (6%)
  starting transfers between devices  19.5 us (5%)
  between operations  14.5 us (4%)
    psum x1, waiting for transfers between devices, per_device(): lax.psum((qkv_part, out_part, gain_part), 'seg')  82.6 us
    psum x1, waiting for transfers between devices, per_device(): grad_hidden = lax.psum(hidden_part, 'mp')  62.2 us
    all_to_all x1, waiting for transfers between devices, per_device(): lax.all_to_all(buffer.reshape(segments, capacity, columns_here), 'seg', s...  59.7 us
    psum x1, blocking collectives, per_device(): lax.psum((qkv_part, out_part, gain_part), 'seg')  22.3 us
    sub x2, matrix products, per_device(): exponent = jnp.where(allowed, jnp.exp(scores - row_top), 0.0)  11.4 us
    gather x2, local copies, waits for them, and re-layouts, per_device(): routed = arrived.reshape(segments * capacity, columns_here)[arrival_slot]  9.59 us
    or x2, other arithmetic, per_device(): allowed = allowed | (listed[:, column:column + 1] == positions[None, :])  9.56 us
    ppermute x2, starting transfers between devices, with_halo(): lax.ppermute(tail, axis, [(i, (i + 1) % count) for i in range(ends)])  9.05 us
  transfers between devices with their start and end apart: 7, of which 6 were waited for; matrix products, arithmetic and copies ran while one was open for 8% of the time, Pallas kernels for 0%

commit v1 on v0

--- a/solution.py
+++ b/solution.py
@@ -158,7 +158,7 @@
     hidden_part = lax.dot_general(
         grad_qkv, flat_weight, (((1,), (1,)), ((), ())), preferred_element_type=jnp.float32
     )
-    grad_hidden = lax.psum(hidden_part, "mp")
+    grad_hidden = jnp.sum(lax.all_gather(hidden_part, "mp"), axis=0)
     scaled = grad_hidden * norm_gain
     full_grads = cotangent.astype(jnp.float32) + inv_rms * (
         scaled - normed * jnp.mean(scaled * normed, axis=1, keepdims=True)

time: 361 us -> 327 us (0.906)
  waiting for transfers between devices: 215 us -> 173 us
  other arithmetic: 33.5 us -> 41.7 us
    psum x1 -> x0, waiting for transfers between devices: 62.2 us -> none  [per_device(): grad_hidden = lax.psum(hidden_part, 'mp')]
    psum x1, waiting for transfers between devices: 82.6 us -> 104 us  [per_device(): lax.psum((qkv_part, out_part, gain_part), 'seg')]
    reduce_sum x0 -> x1, other arithmetic: none -> 7.43 us  [per_device(): grad_hidden = jnp.sum(lax.all_gather(hidden_part, 'mp'), axis=0)]
  transfers between devices with their start and end apart: 7 -> 7, of which waited for: 6 -> 5; matrix products, arithmetic and copies ran while one was open for 8% -> 7% of each run, Pallas kernels for 0% -> 0%
where the time goes in v1:
time: 327 us
  waiting for transfers between devices  173 us (53%)
  other arithmetic  41.7 us (13%)
  matrix products  30.8 us (9%)
  local copies, waits for them, and re-layouts  25.7 us (8%)
  starting transfers between devices  19.6 us (6%)
  blocking collectives  19.6 us (6%)
  between operations  16 us (5%)
    psum x1, waiting for transfers between devices, per_device(): lax.psum((qkv_part, out_part, gain_part), 'seg')  104 us
    all_to_all x1, waiting for transfers between devices, per_device(): lax.all_to_all(buffer.reshape(segments, capacity, columns_here), 'seg', s...  59.7 us
    psum x1, blocking collectives, per_device(): lax.psum((qkv_part, out_part, gain_part), 'seg')  19.6 us
    sub x2, matrix products, per_device(): exponent = jnp.where(allowed, jnp.exp(scores - row_top), 0.0)  10.8 us
    gather x2, local copies, waits for them, and re-layouts, per_device(): routed = arrived.reshape(segments * capacity, columns_here)[arrival_slot]  9.59 us
    or x2, other arithmetic, per_device(): allowed = allowed | (listed[:, column:column + 1] == positions[None, :])  9.56 us
    ppermute x2, starting transfers between devices, with_halo(): lax.ppermute(tail, axis, [(i, (i + 1) % count) for i in range(ends)])  9.19 us
    scatter x1, local copies, waits for them, and re-layouts, per_device(): jnp.zeros((segments * capacity, columns_here), patches.dtype).at[slot_index]  7.9 us
  transfers between devices with their start and end apart: 7, of which 5 were waited for; matrix products, arithmetic and copies ran while one was open for 7% of the time, Pallas kernels for 0%

profile of v1, /device:TPU:0, one launch (start us, length us, event | category | flops | bytes accessed | tf_op | source)
XLA Modules:
  0.0 326.7 jit_solution(14377422828461093244)
XLA Ops:
  8.8 2.3 reduce-window.6
  13.0 7.9 %scatter_custom_fusion = bf16[2048,768]{1,0:T(8,128)(2,1)} fusion(s32[1024]{0:T(1024)S(1)} %compare_select_fusion.1, bf16[1024,768]{1,0:T(8,128)(2,1)} %param.18, bf16[]{:T(256)} %constant.136.clone.1), kind=kCustom, calls=%fused_computation.33 | custom fusion | bytes 3146240 | tf_op jit(solution)/shard_map/scatter | solution.py:56
  20.9 7.4 %all-to-all-start = ((bf16[8,256,768]{2,1,0:T(8,128)(2,1)}), bf16[8,256,768]{2,1,0:T(8,128)(2,1)}, u32[]{:S(2)}, u32[]{:S(2)}) async-start(bf16[8,256,768]{2,1,0:T(8,128)(2,1)} %bitcast.154), calls=%async_computation | async-start | bytes 6291456 | tf_op jit(solution)/shard_map/all_to_all | solution.py:58
  29.9 4.8 %compare_or_fusion.1 = pred[512,768]{1,0:T(8,128)(4,1)} fusion(s32[768]{0:T(1024)S(1)} %iota_add_fusion.1, s32[512]{0:T(512)S(1)} %bitcast.204, s32[512]{0:T(512)S(1)} %bitcast.205, s32[512]{0:T(512)S(1)} %bitcast.206, s32[512]{0:T(512)S(1)} %bitcast.207, s32[512]{0:T(512)S(1)} %bitcast.208, s32[512]{0:T(512)S(1)} %bitcast.211, s32[512]{0:T(512)S(1)} %bitcast.212, ...), kind=kLoop, calls=%fused_computation.36 | loop fusion | flops 12189696 | bytes 429056 | tf_op jit(solution)/shard_map/or | solution.py:105
  34.7 4.8 %compare_or_fusion = pred[512,768]{1,0:T(8,128)(4,1)} fusion(s32[768]{0:T(1024)S(1)} %iota_add_fusion, s32[512]{0:T(512)S(1)} %bitcast.210, s32[512]{0:T(512)S(1)} %bitcast.209, s32[512]{0:T(512)S(1)} %bitcast.191, s32[512]{0:T(512)S(1)} %bitcast.192, s32[512]{0:T(512)S(1)} %bitcast.193, s32[512]{0:T(512)S(1)} %bitcast.194, s32[512]{0:T(512)S(1)} %bitcast.195, ...), kind=kLoop, calls=%fused_computation.35 | loop fusion | flops 12189696 | bytes 429056 | tf_op jit(solution)/shard_map/or | solution.py:105
  39.5 59.7 %all-to-all-done = bf16[8,256,768]{2,1,0:T(8,128)(2,1)} async-done(((bf16[8,256,768]{2,1,0:T(8,128)(2,1)}), bf16[8,256,768]{2,1,0:T(8,128)(2,1)}, u32[]{:S(2)}, u32[]{:S(2)}) %all-to-all-start) | async-done | bytes 3145760 | tf_op jit(solution)/shard_map/all_to_all | solution.py:58
  99.1 7.9 %gather_fusion = bf16[1024,768]{1,0:T(8,128)(2,1)} fusion(bf16[2048,768]{1,0:T(8,128)(2,1)} %bitcast.3, s32[1024]{0:T(1024)S(1)} %fusion.43), kind=kCustom, calls=%fused_computation | custom fusion | bytes 3149824 | tf_op jit(solution)/shard_map/gather | solution.py:65
  114.0 4.7 %collective-permute-start = (bf16[128,384]{0,1:T(8,128)(2,1)S(1)}, bf16[128,384]{0,1:T(8,128)(2,1)S(1)}, u32[]{:S(2)}, u32[]{:S(2)}) collective-permute-start(bf16[128,384]{0,1:T(8,128)(2,1)S(1)} %get-tuple-element.62), channel_id=1, source_target_pairs={{0,4},{4,8},{8,12},{12,16},{16,20},{20,24},{24,28},{1,5},{5,9},{9,... | collective-permute-start | bytes 294920 | tf_op jit(solution)/shard_map/ppermute | solution.py:19
  120.9 4.4 %fusion.57 = (f32[3,512]{1,0:T(4,128)S(1)}, f32[3,512,768]{2,1,0:T(8,128)}) fusion(pred[512,768]{1,0:T(8,128)(4,1)S(1)} %copy-done.9, bf16[512,3,64]{0,2,1:T(8,128)(2,1)S(1)} %bitcast.178, bf16[768,2,3,64]{0,3,2,1:T(8,128)(2,1)S(1)} %bitcast.159), kind=kOutput, calls=%fused_computation.108 | convolution fusion | flops 309068544 | bytes 6494208 | tf_op jit(solution)/shard_map/sub | solution.py:112
  125.3 2.7 fusion.17
  130.1 6.4 %fusion.58 = (f32[3,512]{1,0:T(4,128)}, f32[3,512,768]{2,1,0:T(8,128)}) fusion(pred[512,768]{1,0:T(8,128)(4,1)} %compare_or_fusion, bf16[512,3,64]{0,2,1:T(8,128)(2,1)} %bitcast.180, bf16[768,2,3,64]{0,3,2,1:T(8,128)(2,1)S(1)} %bitcast.163), kind=kOutput, calls=%fused_computation.109 | convolution fusion | flops 309068544 | bytes 6494208 | tf_op jit(solution)/shard_map/sub | solution.py:112
  136.5 2.7 fusion.18
  147.1 4.5 %collective-permute-start.2 = (f32[128,384]{0,1:T(8,128)S(1)}, f32[128,384]{0,1:T(8,128)S(1)}, u32[]{:S(2)}, u32[]{:S(2)}) collective-permute-start(f32[128,384]{0,1:T(8,128)S(1)} %slice.336), channel_id=1, source_target_pairs={{0,4},{4,8},{8,12},{12,16},{16,20},{20,24},{24,28},{1,5},{5,9},{9,... | collective-permute-start | bytes 589832 | tf_op jit(solution)/shard_map/ppermute | solution.py:19
  152.4 2.3 collective-permute-done.2
  157.4 6.2 %collective-permute-done.3 = f32[128,384]{0,1:T(8,128)S(1)} collective-permute-done((f32[128,384]{0,1:T(8,128)S(1)}, f32[128,384]{0,1:T(8,128)S(1)}, u32[]{:S(2)}, u32[]{:S(2)}) %collective-permute-start.3) | collective-permute-done | bytes 196640 | tf_op jit(solution)/shard_map/ppermute | solution.py:21
  163.8 2.4 fusion.28
  167.1 4.2 %fusion.29 = f32[1024,768]{1,0:T(8,128)} fusion(bf16[768,576]{0,1:T(8,128)(2,1)} %bitcast.222, bf16[1024,384]{0,1:T(8,128)(2,1)S(1)} %convert.16, bf16[512,192]{0,1:T(8,128)(2,1)S(1)} %bitcast.183, bf16[512,192]{0,1:T(8,128)(2,1)S(1)} %bitcast.185), kind=kOutput, calls=%fused_computation.57 | convolution fusion | flops 909508608 | bytes 5210112 | tf_op jit(solution)/shard_map/dot_general | solution.py:158
  171.8 103.8 %all-reduce.4.cloned.1.call-done = (f32[768,576]{0,1:T(8,128)}, f32[192,768]{1,0:T(8,128)}) async-done(((f32[768,576]{0,1:T(8,128)}, f32[192,768]{1,0:T(8,128)}), (f32[768,576]{0,1:T(8,128)}, f32[192,768]{1,0:T(8,128)})) %all-reduce.4.cloned.1.call-update) | async-done | bytes 2359312 | tf_op jit(solution)/shard_map/psum | solution.py:170
  277.6 2.8 broadcast_multiply_fusion.1
  280.4 7.4 %reduce_sum.87 = f32[1024,768]{1,0:T(8,128)} reduce(f32[4,1024,768]{2,1,0:T(8,128)} %bitcast.153, f32[]{:T(128)} %constant.140.clone.1), dimensions={0}, to_apply=%region_11.12 | reduce | flops 2359296 | bytes 15728644 | tf_op jit(solution)/shard_map/reduce_sum | solution.py:161
  287.9 3.5 %copy.20 = f32[1024,768]{0,1:T(8,128)} copy(f32[1024,768]{1,0:T(8,128)} %reduce_sum.87) | data formatting | bytes 6291456 | tf_op jit(solution)/shard_map/reduce_sum | solution.py:161
  291.4 5.2 %multiply_reduce_fusion = (f32[768]{0:T(1024)S(1)}, f32[1024]{0:T(1024)S(1)}, f32[1024,768]{0,1:T(8,128)}) fusion(f32[1024,768]{0,1:T(8,128)} %copy.20, f32[1024,768]{0,1:T(8,128)} %copy-done.1, f32[768]{0:T(1024)S(1)} %copy-done.17), kind=kLoop, calls=%fused_computation.14 | loop fusion | flops 3930368 | bytes 9447424 | tf_op jit(solution)/shard_map/reduce_sum | solution.py:168
  296.6 19.6 %psum.23 = f32[192]{0:T(256)S(1)} all-reduce(f32[192]{0:T(256)S(1)} %dynamic_slice.7), channel_id=1, replica_groups=mesh['seg'=8,'mp'=4] {'seg'}, use_global_device_ids=true, to_apply=%region_16.17 | all-reduce | flops 192 | bytes 1536 | tf_op jit(solution)/shard_map/psum | solution.py:170
  316.8 2.5 fusion.22
  (104 shorter events, 30.6 us)
Async XLA Ops:
  8.0 20.5 %copy-start = (bf16[1024,768]{1,0:T(8,128)(2,1)S(1)}, bf16[1024,768]{1,0:T(8,128)(2,1)}, u32[]{:S(2)}) copy-start(bf16[1024,768]{1,0:T(8,128)(2,1)} %param.27) | copy-start | bytes 4718596
  20.9 7.5 %copy-start.19 = (s32[1024]{0:T(1024)S(1)}, s32[1024]{0:T(1024)}, u32[]{:S(2)}) copy-start(s32[1024]{0:T(1024)} %param.20) | copy-start | bytes 12292
  20.9 7.5 %copy-start.12 = (s32[1024,16]{0,1:T(8,128)S(1)}, s32[1024,16]{0,1:T(8,128)}, u32[]{:S(2)}) copy-start(s32[1024,16]{0,1:T(8,128)} %param.22) | copy-start | bytes 196612
  20.9 7.6 %copy-start.21 = (bf16[192,768]{1,0:T(8,128)(2,1)S(1)}, bf16[192,768]{1,0:T(8,128)(2,1)}, u32[]{:S(2)}) copy-start(bf16[192,768]{1,0:T(8,128)(2,1)} %param.26) | copy-start | bytes 884740
  20.9 78.2 %all-to-all-start = ((bf16[8,256,768]{2,1,0:T(8,128)(2,1)}), bf16[8,256,768]{2,1,0:T(8,128)(2,1)}, u32[]{:S(2)}, u32[]{:S(2)}) async-start(bf16[8,256,768]{2,1,0:T(8,128)(2,1)} %bitcast.154), calls=%async_computation | async-start | bytes 6291456 | tf_op jit(solution)/shard_map/all_to_all | solution.py:58
  28.3 247.3 %all-reduce.4.cloned.1.call-start = ((), (), s32[]{:S(2)}) async-start(), calls=%async_computation.2 | async-start | bytes 4718592 | tf_op jit(solution)/shard_map/psum | solution.py:170
  107.0 1.8 copy-start.16
  107.0 1.8 copy-start.18
  112.6 8.3 %copy-start.9 = (pred[512,768]{1,0:T(8,128)(4,1)S(1)}, pred[512,768]{1,0:T(8,128)(4,1)}, u32[]{:S(2)}) copy-start(pred[512,768]{1,0:T(8,128)(4,1)} %compare_or_fusion.1) | copy-start | bytes 1179652
  112.6 6.9 %collective-permute-start.1 = (bf16[128,384]{0,1:T(8,128)(2,1)S(1)}, bf16[128,384]{0,1:T(8,128)(2,1)S(1)}, u32[]{:S(2)}, u32[]{:S(2)}) collective-permute-start(bf16[128,384]{0,1:T(8,128)(2,1)S(1)} %get-tuple-element.61), channel_id=1, source_target_pairs={{4,0},{8,4},{12,8},{16,12},{20,16},{24,20},{28,24},{5,1},{9,5},{13... | collective-permute-start | bytes 294920 | tf_op jit(solution)/shard_map/ppermute | solution.py:21
  114.0 6.8 %collective-permute-start = (bf16[128,384]{0,1:T(8,128)(2,1)S(1)}, bf16[128,384]{0,1:T(8,128)(2,1)S(1)}, u32[]{:S(2)}, u32[]{:S(2)}) collective-permute-start(bf16[128,384]{0,1:T(8,128)(2,1)S(1)} %get-tuple-element.62), channel_id=1, source_target_pairs={{0,4},{4,8},{8,12},{12,16},{16,20},{20,24},{24,28},{1,5},{5,9},{9,... | collective-permute-start | bytes 294920 | tf_op jit(solution)/shard_map/ppermute | solution.py:19
  119.5 5.8 %copy-start.6 = (bf16[512,192]{0,1:T(8,128)(2,1)}, bf16[512,192]{0,1:T(8,128)(2,1)S(1)}, u32[]{:S(2)}) copy-start(bf16[512,192]{0,1:T(8,128)(2,1)S(1)} %get-tuple-element.64) | copy-start | bytes 589828
  125.3 2.7 copy-start.13
  136.5 2.7 copy-start.4
  139.2 2.3 copy-start.3
  139.3 2.3 copy-start.15
  139.8 4.6 %slice-start = ((s8[4718592]{0:T(1024)(128)(4,1)}), s8[524288]{0:T(1024)(128)(4,1)S(1)}, s32[]{:S(2)}) async-start(s8[4718592]{0:T(1024)(128)(4,1)} %bitcast.155), calls=%async_computation.3 | async-start | bytes 1048576
  141.6 2.8 slice-start.1
  144.3 19.4 %copy-start.10 = (bf16[3,64,512]{2,1,0:T(8,128)(2,1)}, bf16[3,64,512]{2,1,0:T(8,128)(2,1)S(1)}, u32[]{:S(2)}) copy-start(bf16[3,64,512]{2,1,0:T(8,128)(2,1)S(1)} %convolution_convert_fusion.2) | copy-start | bytes 589828
  147.1 9.0 %copy-start.5 = (bf16[3,64,512]{2,1,0:T(8,128)(2,1)S(1)}, bf16[3,64,512]{2,1,0:T(8,128)(2,1)}, u32[]{:S(2)}) copy-start(bf16[3,64,512]{2,1,0:T(8,128)(2,1)} %get-tuple-element.106) | copy-start | bytes 589828
  147.1 7.6 %collective-permute-start.2 = (f32[128,384]{0,1:T(8,128)S(1)}, f32[128,384]{0,1:T(8,128)S(1)}, u32[]{:S(2)}, u32[]{:S(2)}) collective-permute-start(f32[128,384]{0,1:T(8,128)S(1)} %slice.336), channel_id=1, source_target_pairs={{0,4},{4,8},{8,12},{12,16},{16,20},{20,24},{24,28},{1,5},{5,9},{9,... | collective-permute-start | bytes 589832 | tf_op jit(solution)/shard_map/ppermute | solution.py:19
  154.8 8.8 %collective-permute-start.3 = (f32[128,384]{0,1:T(8,128)S(1)}, f32[128,384]{0,1:T(8,128)S(1)}, u32[]{:S(2)}, u32[]{:S(2)}) collective-permute-start(f32[128,384]{0,1:T(8,128)S(1)} %get-tuple-element.59), channel_id=1, source_target_pairs={{4,0},{8,4},{12,8},{16,12},{20,16},{24,20},{28,24},{5,1},{9,5},{13... | collective-permute-start | bytes 589832 | tf_op jit(solution)/shard_map/ppermute | solution.py:21
  156.1 7.7 %copy-start.2 = (f32[1024,768]{0,1:T(8,128)S(1)}, f32[1024,768]{0,1:T(8,128)}, u32[]{:S(2)}) copy-start(f32[1024,768]{0,1:T(8,128)} %copy-done.1) | copy-start | bytes 9437188
  166.2 114.2 %all-gather.3.cloned.1.call-start = ((), (), s32[]{:S(2)}) async-start(), calls=%async_computation.1 | async-start | bytes 15728640 | tf_op jit(solution)/shard_map/all_gather | solution.py:161
  (7 other events, 8.7 us)
Sparse Core Ops, SparseCore 0:
  166.4 109.2 all-reduce.3
Sparse Core Ops, SparseCore 1:
  171.5 82.6 all-gather.2
